TPU v7x, 32 devices: a whole 2x2x4 slice. The times are simulated.
32 devices in a mesh: section: 4 (over y, core), seq: 8 (over z, x).
Axes of the slice: x: 2, y: 2, z: 4, core: 2. Of those that a mesh axis runs over, the one named last changes fastest.
Arguments:
- context: bfloat16 [2048, 8192], P('seq'), may hold values from -24 to 24, as said below
- memory: bfloat16 [512, 8192], P('seq'), may hold values from -24 to 24, as said below
- query_weight: bfloat16 [8192, 4096], P(None, 'section'), may hold values from -0.0625 to 0.0625
- key_weight: bfloat16 [8192, 512], P('seq', 'section'), may hold values from -0.0625 to 0.0625
- value_weight: bfloat16 [8192, 512], P('seq', 'section'), may hold values from -0.0625 to 0.0625
- query_down_map: bfloat16 [8192, 128], replicated, may hold values from -0.0625 to 0.0625
- query_up_map: bfloat16 [128, 4096], P(None, 'section'), may hold values from -0.5 to 0.5
- value_down_map: bfloat16 [8192, 128], P('seq'), may hold values from -0.0625 to 0.0625
- value_up_map: bfloat16 [128, 512], P(None, 'section'), may hold values from -0.5 to 0.5
- output_weight: bfloat16 [4096, 8192], P('section', 'seq'), may hold values from -1 to 1
- decoder_gain: float32 [8192], P('seq'), may hold values from 0.25 to 1.75
- document_slots: int32 [8], replicated, may hold values from 1 to 320, 512 in all
- normed_gradient: bfloat16 [512, 8192], P('section', 'seq'), may hold values from -6 to 6
Outputs:
- normed: bfloat16 [512, 8192], P('section', 'seq')
- grad_qa: float32 [8192, 128], P(('section', 'seq'))
- grad_va: float32 [8192, 128], P(('section', 'seq'))
- query_up_gradient: float32 [128, 4096], P(None, 'section')
- value_up_gradient: float32 [128, 512], P(None, 'section')
Inputs may be any that keep to these rules, and one draw needn't show every extreme that they name: `context`: values of the normed inputs lie in this range. `memory`: values of the normed inputs lie in this range. Documents lie end to end in order; document d has document_slots[d] memory slots and 4 document_slots[d] context tokens; the counts sum to 512.
All inputs are finite; a program needn't handle non-finite values.
Results may differ from a plain program's by a relative error of at most 0.014.
The roundings to bfloat16 on the way count: a program that leaves them out, or rounds other values in their place, can miss the bound.
Values may be sent and summed in bfloat16 or wider, within the bound.
No kernel may reach another device: no remote copies, remote signals or barrier semaphores. Data moves between devices by JAX's collectives and lax.ppermute only.
A program may use at most 192 MiB of HBM per device.

v0:
```python
import jax
import jax.numpy as jnp
from jax import lax
from jax.sharding import PartitionSpec as P

MODEL_DIM = 8192
adapter_scale = 0.25
epsilon = 1e-05
mask_fill = -1e30


def doc_index(units, doc_ends):
    return jnp.sum((units[:, None] >= doc_ends[None, :]).astype(jnp.int32), axis=1)


def leading_contract(left, right):
    return lax.dot_general(
        left, right, (((0,), (0,)), ((), ())), preferred_element_type=jnp.float32
    )


def trailing_contract(left, right):
    return lax.dot_general(
        left, right, (((1,), (1,)), ((), ())), preferred_element_type=jnp.float32
    )


def body(
    context,
    memory,
    query_weight,
    key_weight,
    value_weight,
    query_down_map,
    query_up_map,
    value_down_map,
    value_up_map,
    output_weight,
    decoder_gain,
    document_slots,
    normed_gradient,
):
    tok_dev = context.shape[0]
    slot_dev = memory.shape[0]
    keys_dev = tok_dev + slot_dev
    seq_size = lax.axis_size("seq")
    seq_index = lax.axis_index("seq")
    section_extent = lax.axis_size("section")
    head_dim = key_weight.shape[1]
    group_heads = query_weight.shape[1] // head_dim
    every_row = jnp.concatenate([context, memory], axis=0)
    key_portion = lax.all_gather(key_weight, "seq", axis=0, tiled=True)
    value_fragment = lax.all_gather(value_weight, "seq", axis=0, tiled=True)
    adapter_portion = lax.all_gather(value_down_map, "seq", axis=0, tiled=True)
    combined_rows = jnp.concatenate([key_portion, value_fragment, adapter_portion], axis=1)
    projected = jnp.dot(every_row, combined_rows, preferred_element_type=jnp.float32)
    query_reduced = jnp.dot(memory, query_down_map, preferred_element_type=jnp.float32).astype(
        jnp.bfloat16
    )
    value_reduced = projected[:, 2 * head_dim :].astype(jnp.bfloat16)
    query_rows_out = (
        jnp.dot(memory, query_weight, preferred_element_type=jnp.float32)
        + adapter_scale * jnp.dot(query_reduced, query_up_map, preferred_element_type=jnp.float32)
    ).astype(jnp.bfloat16)
    keys_local = projected[:, :head_dim].astype(jnp.bfloat16)
    values_local = (
        projected[:, head_dim : 2 * head_dim]
        + adapter_scale * jnp.dot(value_reduced, value_up_map, preferred_element_type=jnp.float32)
    ).astype(jnp.bfloat16)
    keys_all, value_rows_all = (
        lax.all_gather(keys_local, "seq", axis=0, tiled=True),
        lax.all_gather(values_local, "seq", axis=0, tiled=True),
    )
    key_rank = jnp.arange(seq_size * keys_dev, dtype=jnp.int32)
    key_owner = key_rank // keys_dev
    owner_valid = jnp.ones(key_rank.shape, dtype=bool)
    doc_ends = jnp.cumsum(document_slots)
    offset = key_rank % keys_dev
    is_context = offset < tok_dev
    key_unit = jnp.where(
        is_context, (key_owner * tok_dev + offset) // 4, key_owner * slot_dev + offset - tok_dev
    )
    key_doc = doc_index(key_unit, doc_ends)
    slot_unit = seq_index * slot_dev + jnp.arange(slot_dev, dtype=jnp.int32)
    row_unit = jnp.repeat(slot_unit, group_heads)
    row_doc = doc_index(row_unit, doc_ends)
    allowed = (
        (key_doc[None, :] == row_doc[:, None])
        & (is_context[None, :] | (key_unit[None, :] <= row_unit[:, None]))
        & owner_valid[None, :]
    )
    score_scale = head_dim ** (-0.5)
    query_rows = query_rows_out.reshape(slot_dev * group_heads, head_dim)
    scores = jnp.where(allowed, trailing_contract(query_rows, keys_all) * score_scale, mask_fill)
    row_top = jnp.max(scores, axis=1, keepdims=True)
    exponent = jnp.exp(scores - row_top)
    probability = exponent / jnp.sum(exponent, axis=1, keepdims=True)
    prob_low = probability.astype(jnp.bfloat16)
    attended = (
        jnp.dot(prob_low, value_rows_all, preferred_element_type=jnp.float32)
        .reshape(slot_dev, group_heads * head_dim)
        .astype(jnp.bfloat16)
    )
    slots_all = lax.all_gather(attended, "seq", axis=0, tiled=True)
    hidden = lax.psum_scatter(
        jnp.dot(slots_all, output_weight, preferred_element_type=jnp.float32),
        "section",
        scatter_dimension=0,
        tiled=True,
    )
    total_slots = slot_dev * seq_size
    weighted = total_slots ** (-0.5) * normed_gradient.astype(jnp.float32) * decoder_gain[None, :]
    square_sum, cross_sum = lax.psum(
        (jnp.sum(hidden * hidden, axis=1), jnp.sum(weighted * hidden, axis=1)), "seq"
    )
    inv_rms = lax.rsqrt(square_sum / MODEL_DIM + epsilon)
    normed = (hidden * inv_rms[:, None] * decoder_gain[None, :]).astype(jnp.bfloat16)
    d_hidden = (
        inv_rms[:, None] * weighted - hidden * (inv_rms**3 * cross_sum / MODEL_DIM)[:, None]
    ).astype(jnp.bfloat16)
    grads_all = lax.all_gather(d_hidden, "section", axis=0, tiled=True)
    d_attended = lax.psum_scatter(
        trailing_contract(grads_all, output_weight), "seq", scatter_dimension=0, tiled=True
    ).astype(jnp.bfloat16)
    grad_rows_local = d_attended.reshape(slot_dev * group_heads, head_dim)
    d_probs = trailing_contract(grad_rows_local, value_rows_all)
    center = jnp.sum(probability * d_probs, axis=1, keepdims=True)
    d_scores = (probability * (d_probs - center)).astype(jnp.bfloat16)
    query_gradient = (
        (score_scale * jnp.dot(d_scores, keys_all, preferred_element_type=jnp.float32))
        .reshape(slot_dev, group_heads * head_dim)
        .astype(jnp.bfloat16)
    )
    value_gradient = lax.psum_scatter(
        leading_contract(prob_low, grad_rows_local), "seq", scatter_dimension=0, tiled=True
    ).astype(jnp.bfloat16)
    query_up_portion = adapter_scale * leading_contract(query_reduced, query_gradient)
    value_up_portion = adapter_scale * leading_contract(value_reduced, value_gradient)
    query_up_gradient, value_up_gradient = lax.psum((query_up_portion, value_up_portion), "seq")
    query_portion = adapter_scale * trailing_contract(query_gradient, query_up_map)
    value_portion = adapter_scale * trailing_contract(value_gradient, value_up_map)
    query_backward, value_backward = lax.psum((query_portion, value_portion), "section")
    query_backward = query_backward.astype(jnp.bfloat16)
    value_backward = value_backward.astype(jnp.bfloat16)
    model_width = memory.shape[1]
    section_columns = model_width // section_extent
    section_index = lax.axis_index("section")
    memory_cols = lax.dynamic_slice_in_dim(
        memory, section_index * section_columns, section_columns, 1
    )
    row_cols = lax.dynamic_slice_in_dim(
        every_row, section_index * section_columns, section_columns, 1
    )
    grad_qa, grad_va = (
        lax.psum_scatter(
            leading_contract(memory_cols, query_backward), "seq", scatter_dimension=0, tiled=True
        ),
        lax.psum_scatter(
            leading_contract(row_cols, value_backward), "seq", scatter_dimension=0, tiled=True
        ),
    )
    return (normed, grad_qa, grad_va, query_up_gradient, value_up_gradient)


def solution(mesh):
    in_specs = (
        P("seq", None),
        P("seq", None),
        P(None, "section"),
        P("seq", "section"),
        P("seq", "section"),
        P(),
        P(None, "section"),
        P("seq", None),
        P(None, "section"),
        P("section", "seq"),
        P("seq"),
        P(),
        P("section", "seq"),
    )
    out_specs = (
        P("section", "seq"),
        P(("section", "seq"), None),
        P(("section", "seq"), None),
        P(None, "section"),
        P(None, "section"),
    )
    return jax.shard_map(body, mesh=mesh, in_specs=in_specs, out_specs=out_specs, check_vma=False)
```

profile of v0, /device:TPU:0, one launch (start us, length us, event | category | flops | bytes accessed | tf_op | source)
XLA Modules:
  0.0 713.7 jit_solution(12109832830738827667)
XLA Ops:
  7.2 0.7 all-gather.6.cloned.1.call-update
  8.0 0.7 all-gather.8.cloned.1.call-update
  8.7 0.7 all-gather.10.cloned.1.call-update
  9.5 2.4 convolution_convert_fusion
  12.1 1.1 convolution_multiply_fusion.1
  13.2 8.8 %fusion.18 = bf16[64,1024]{1,0:T(8,128)(2,1)S(1)} fusion(f32[64,1024]{1,0:T(8,128)S(1)} %convolution_multiply_fusion.1, bf16[64,8192]{1,0:T(8,128)(2,1)S(1)} %copy-done.2, bf16[8192,1024]{1,0:T(8,128)(2,1)} %param.15), kind=kOutput, calls=%fused_computation.25 | convolution fusion | flops 1073872896 | bytes 18219008 | tf_op jit(solution)/shard_map/dot_general | solution.py:62
  22.5 4.7 constant_dynamic-update-slice_fusion.1
  27.2 1.0 constant_dynamic-update-slice_fusion
  28.2 33.8 %all-gather.6.cloned.1.call-done = bf16[8192,128]{1,0:T(8,128)(2,1)} async-done(((bf16[1024,128]{1,0:T(8,128)(2,1)}), bf16[8192,128]{1,0:T(8,128)(2,1)}) %all-gather.6.cloned.1.call-update) | async-done | bytes 2097168 | tf_op jit(solution)/shard_map/all_gather | solution.py:52
  62.0 49.8 %all-gather.8.cloned.1.call-done = bf16[8192,128]{1,0:T(8,128)(2,1)} async-done(((bf16[1024,128]{1,0:T(8,128)(2,1)}), bf16[8192,128]{1,0:T(8,128)(2,1)}) %all-gather.8.cloned.1.call-update) | async-done | bytes 2097168 | tf_op jit(solution)/shard_map/all_gather | solution.py:53
  111.8 49.8 %all-gather.10.cloned.1.call-done = bf16[8192,128]{1,0:T(8,128)(2,1)} async-done(((bf16[1024,128]{1,0:T(8,128)(2,1)}), bf16[8192,128]{1,0:T(8,128)(2,1)}) %all-gather.10.cloned.1.call-update) | async-done | bytes 2097168 | tf_op jit(solution)/shard_map/all_gather | solution.py:54
  161.6 7.2 %fusion.51 = (bf16[320,384]{1,0:T(8,128)(2,1)S(1)}, f32[320,384]{1,0:T(8,128)S(1)}) fusion(bf16[320,8192]{1,0:T(8,128)(2,1)} %constant_dynamic-update-slice_fusion, bf16[8192,128]{1,0:T(8,128)(2,1)} %all-gather.10.cloned.1.call-done, bf16[8192,128]{1,0:T(8,128)(2,1)} %all-gather.8.cloned.1.call-done, bf16[8192,128]{1,0:T(8,128)(2,1)} %all-gather.6.cloned.1.call-done), kind=kOutput, calls=%fused_computation.83 | convolution fusion | flops 2032263168 | bytes 12271616 | tf_op jit(solution)/shard_map/dot_general | solution.py:56
  168.8 32.0 %all_gather.24 = bf16[2560,128]{1,0:T(8,128)(2,1)S(1)} all-gather(bf16[320,128]{1,0:T(8,128)(2,1)S(1)} %slice.14), channel_id=1, replica_groups=mesh['section'=4,'seq'=8] {'seq'}, dimensions={0}, use_global_device_ids=true | all-gather | bytes 737280 | tf_op jit(solution)/shard_map/all_gather | solution.py:71
  201.0 32.0 %all_gather.25 = bf16[2560,128]{1,0:T(8,128)(2,1)S(1)} all-gather(bf16[320,128]{1,0:T(8,128)(2,1)S(1)} %fusion.23), channel_id=1, replica_groups=mesh['section'=4,'seq'=8] {'seq'}, dimensions={0}, use_global_device_ids=true | all-gather | bytes 737280 | tf_op jit(solution)/shard_map/all_gather | solution.py:72
  233.0 2.0 fusion.52
  235.0 0.8 fusion.7
  235.9 1.3 fusion.6
  237.2 2.3 copy-done.1
  239.5 0.8 fusion.19
  240.3 0.7 convert_element_type.63
  241.1 38.3 %all-gather.12.cloned.1.call-done = bf16[512,1024]{1,0:T(8,128)(2,1)} async-done(((bf16[64,1024]{1,0:T(8,128)(2,1)}), bf16[512,1024]{1,0:T(8,128)(2,1)}) %all-gather.12.cloned.1.call-update) | async-done | bytes 1048592 | tf_op jit(solution)/shard_map/all_gather | solution.py:104
  279.4 3.8 fusion.53
  283.2 0.2 all-gather.14.cloned.1.call-start
  283.5 29.8 %reduce-scatter.6.cloned.1.call-done = f32[128,1024]{1,0:T(8,128)} async-done(((f32[512,1024]{1,0:T(8,128)}), f32[128,1024]{1,0:T(8,128)}) %reduce-scatter.6.cloned.1.call-update) | async-done | bytes 524304 | tf_op jit(solution)/shard_map/reduce_scatter | solution.py:105
  313.3 1.2 multiply_reduce_fusion.1
  314.5 21.4 %all-reduce = (f32[128]{0:T(128)S(1)}, f32[128]{0:T(128)S(1)}) all-reduce(f32[128]{0:T(128)S(1)} %get-tuple-element.6, f32[128]{0:T(128)S(1)} %get-tuple-element.5), channel_id=1, replica_groups=mesh['section'=4,'seq'=8] {'seq'}, use_global_device_ids=true, to_apply=%region_7.8 | all-reduce | flops 256 | bytes 2048 | tf_op jit(solution)/shard_map/psum | solution.py:113
  335.9 2.0 subtract_convert_fusion
  338.0 13.1 %all-gather.14.cloned.1.call-done = bf16[512,1024]{1,0:T(8,128)(2,1)} async-done(((bf16[128,1024]{1,0:T(8,128)(2,1)}), bf16[512,1024]{1,0:T(8,128)(2,1)}) %all-gather.14.cloned.1.call-update) | async-done | bytes 1048592 | tf_op jit(solution)/shard_map/all_gather | solution.py:121
  351.1 3.8 fusion.54
  355.0 68.5 %reduce-scatter.8.cloned.1.call-done = f32[64,1024]{1,0:T(8,128)} async-done(((f32[512,1024]{1,0:T(8,128)}), f32[64,1024]{1,0:T(8,128)}) %reduce-scatter.8.cloned.1.call-update) | async-done | bytes 262160 | tf_op jit(solution)/shard_map/reduce_scatter | solution.py:122
  423.5 1.0 convert_element_type.67
  424.6 4.4 fusion.12
  429.1 3.8 multiply_reduce_fusion
  432.9 0.4 slice-done.1
  433.4 1.1 fusion.17
  434.5 1.0 convolution_multiply_fusion
  435.6 57.8 %reduce-scatter.12.cloned.1.call-done = f32[320,128]{1,0:T(8,128)} async-done(((f32[2560,128]{1,0:T(8,128)}), f32[320,128]{1,0:T(8,128)}) %reduce-scatter.12.cloned.1.call-update) | async-done | bytes 163856 | tf_op jit(solution)/shard_map/reduce_scatter | solution.py:134
  493.4 1.8 convolution_multiply_fusion.4
  495.2 0.2 convolution_multiply_fusion.5
  495.4 1.1 convolution_multiply_fusion.2
  496.5 12.6 %all-reduce.7 = (bf16[64,128]{1,0:T(8,128)(2,1)S(1)}, bf16[320,128]{1,0:T(8,128)(2,1)S(1)}) all-reduce(f32[64,128]{1,0:T(8,128)S(1)} %convolution_multiply_fusion.5, f32[320,128]{1,0:T(8,128)S(1)} %convolution_multiply_fusion.2), channel_id=1, replica_groups=mesh['section'=4,'seq'=8] {'section'}, use_global_device_ids=true, to_apply=%region_12.13 | all-reduce | flops 49152 | bytes 294912 | tf_op jit(solution)/shard_map/psum | solution.py:142
  509.1 2.9 fusion.10
  512.1 2.3 fusion.24
  514.5 55.1 %all-reduce.6.cloned.1.call-done = (f32[128,1024]{1,0:T(8,128)}, f32[128,128]{1,0:T(8,128)}) async-done(((f32[128,1024]{1,0:T(8,128)}, f32[128,128]{1,0:T(8,128)}), (f32[128,1024]{1,0:T(8,128)}, f32[128,128]{1,0:T(8,128)})) %all-reduce.6.cloned.1.call-update) | async-done | bytes 589840 | tf_op jit(solution)/shard_map/psum | solution.py:139
  569.6 67.1 %reduce-scatter.14.cloned.1.call-done = f32[256,128]{1,0:T(8,128)} async-done(((f32[2048,128]{1,0:T(8,128)}), f32[256,128]{1,0:T(8,128)}) %reduce-scatter.14.cloned.1.call-update) | async-done | bytes 131088 | tf_op jit(solution)/shard_map/reduce_scatter | solution.py:158
  636.7 67.1 %reduce-scatter.10.cloned.1.call-done = f32[256,128]{1,0:T(8,128)} async-done(((f32[2048,128]{1,0:T(8,128)}), f32[256,128]{1,0:T(8,128)}) %reduce-scatter.10.cloned.1.call-update) | async-done | bytes 131088 | tf_op jit(solution)/shard_map/reduce_scatter | solution.py:155
  703.8 1.9 copy.25
  705.7 1.5 copy.26
  (60 shorter events, 1.7 us)
Async XLA Ops:
  7.2 272.2 %copy-start = (bf16[1024,1024]{1,0:T(8,128)(2,1)S(1)}, bf16[1024,1024]{1,0:T(8,128)(2,1)}, u32[]{:S(2)}) copy-start(bf16[1024,1024]{1,0:T(8,128)(2,1)} %param.22) | copy-start | bytes 6291460
  7.2 6.0 copy-start.2
  7.2 54.8 %all-gather.6.cloned.1.call-start = ((), (), s32[]{:S(2)}) async-start(), calls=%async_computation.5 | async-start | bytes 2359296 | tf_op jit(solution)/shard_map/all_gather | solution.py:52
  7.9 103.9 %all-gather.8.cloned.1.call-start = ((), (), s32[]{:S(2)}) async-start(), calls=%async_computation.6 | async-start | bytes 2359296 | tf_op jit(solution)/shard_map/all_gather | solution.py:53
  8.7 152.9 %all-gather.10.cloned.1.call-start = ((), (), s32[]{:S(2)}) async-start(), calls=%async_computation.7 | async-start | bytes 2359296 | tf_op jit(solution)/shard_map/all_gather | solution.py:54
  9.4 270.0 %all-gather.12.cloned.1.call-start = ((), (), s32[]{:S(2)}) async-start(), calls=%async_computation.8 | async-start | bytes 1179648 | tf_op jit(solution)/shard_map/all_gather | solution.py:104
  13.2 8.9 %copy-start.11 = (s32[8]{0:T(128)S(1)}, s32[8]{0:T(128)}, u32[]{:S(2)}) copy-start(s32[8]{0:T(128)} %param.24) | copy-start | bytes 100
  28.2 172.6 %copy-start.9 = (bf16[128,128]{1,0:T(8,128)(2,1)S(1)}, bf16[128,128]{1,0:T(8,128)(2,1)}, u32[]{:S(2)}) copy-start(bf16[128,128]{1,0:T(8,128)(2,1)} %param.21) | copy-start | bytes 98308
  168.8 66.3 %copy-start.8 = (bf16[320,384]{1,0:T(8,128)(2,1)}, bf16[320,384]{1,0:T(8,128)(2,1)S(1)}, u32[]{:S(2)}) copy-start(bf16[320,384]{1,0:T(8,128)(2,1)S(1)} %get-tuple-element.17) | copy-start | bytes 737284
  200.8 34.2 %copy-start.4 = (bf16[2560,128]{1,0:T(8,128)(2,1)}, bf16[2560,128]{1,0:T(8,128)(2,1)S(1)}, u32[]{:S(2)}) copy-start(bf16[2560,128]{1,0:T(8,128)(2,1)S(1)} %all_gather.24) | copy-start | bytes 1966084
  233.0 4.2 copy-start.3
  237.2 2.3 copy-start.1
  240.3 43.2 %copy-start.10 = (f32[1024]{0:T(1024)S(1)}, f32[1024]{0:T(1024)}, u32[]{:S(2)}) copy-start(f32[1024]{0:T(1024)} %param.23) | copy-start | bytes 12292
  240.3 73.0 %copy-start.7 = (bf16[128,1024]{1,0:T(8,128)(2,1)S(1)}, bf16[128,1024]{1,0:T(8,128)(2,1)}, u32[]{:S(2)}) copy-start(bf16[128,1024]{1,0:T(8,128)(2,1)} %param.25) | copy-start | bytes 786436
  241.1 72.2 %reduce-scatter.6.cloned.1.call-start = ((), (), s32[]{:S(2)}) async-start(), calls=%async_computation.9 | async-start | bytes 2621440 | tf_op jit(solution)/shard_map/reduce_scatter | solution.py:105
  283.2 67.9 %all-gather.14.cloned.1.call-start = ((), (), s32[]{:S(2)}) async-start(), calls=%async_computation.10 | async-start | bytes 1310720 | tf_op jit(solution)/shard_map/all_gather | solution.py:121
  337.9 85.6 %reduce-scatter.8.cloned.1.call-start = ((), (), s32[]{:S(2)}) async-start(), calls=%async_computation.11 | async-start | bytes 2359296 | tf_op jit(solution)/shard_map/reduce_scatter | solution.py:122
  355.0 138.4 %reduce-scatter.12.cloned.1.call-start = ((), (), s32[]{:S(2)}) async-start(), calls=%async_computation.13 | async-start | bytes 1474560 | tf_op jit(solution)/shard_map/reduce_scatter | solution.py:134
  429.0 3.9 slice-start
  429.0 140.6 %all-reduce.6.cloned.1.call-start = ((), (), s32[]{:S(2)}) async-start(), calls=%async_computation.15 | async-start | bytes 1179648 | tf_op jit(solution)/shard_map/psum | solution.py:139
  429.1 4.2 slice-start.1
  429.1 4.3 copy-start.5
  433.4 61.8 %copy-start.6 = (bf16[128,1024]{1,0:T(8,128)(2,1)S(1)}, bf16[128,1024]{1,0:T(8,128)(2,1)}, u32[]{:S(2)}) copy-start(bf16[128,1024]{1,0:T(8,128)(2,1)} %param.19) | copy-start | bytes 786436
  495.2 141.5 %reduce-scatter.14.cloned.1.call-start = ((), (), s32[]{:S(2)}) async-start(), calls=%async_computation.14 | async-start | bytes 1179648 | tf_op jit(solution)/shard_map/reduce_scatter | solution.py:158
  512.1 191.7 %reduce-scatter.10.cloned.1.call-start = ((), (), s32[]{:S(2)}) async-start(), calls=%async_computation.12 | async-start | bytes 1179648 | tf_op jit(solution)/shard_map/reduce_scatter | solution.py:155
Sparse Core Ops, SparseCore 0:
  10.1 51.8 all-gather.5
  64.1 47.6 all-gather.7
  113.9 47.6 all-gather.9
  241.2 38.1 all-gather.11
  283.4 29.8 reduce-scatter.5
  338.1 13.0 all-gather.13
  355.1 68.3 reduce-scatter.7
  429.1 64.1 reduce-scatter.11
  497.3 72.2 all-reduce.5
  573.4 63.2 reduce-scatter.13
  640.7 63.1 reduce-scatter.9
where the time goes:
time: 714 us
  waiting for transfers between devices  532 us (75%)
  blocking collectives  98 us (14%)
  matrix products  48.8 us (7%)
  between operations  14.2 us (2%)
  local copies, waits for them, and re-layouts  13 us (2%)
    reduce_scatter x1, waiting for transfers between devices, body(): lax.psum_scatter(trailing_contract(grads_all, output_weight), 'seq', scat...  68.5 us
    reduce_scatter x1, waiting for transfers between devices, body(): lax.psum_scatter(leading_contract(memory_cols, query_backward), 'seq', sc...  67.1 us
    reduce_scatter x1, waiting for transfers between devices, body(): lax.psum_scatter(leading_contract(row_cols, value_backward), 'seq', scatt...  67.1 us
    reduce_scatter x1, waiting for transfers between devices, body(): lax.psum_scatter(leading_contract(prob_low, grad_rows_local), 'seq', scat...  57.8 us
    psum x1, waiting for transfers between devices, body(): lax.psum((query_up_portion, value_up_portion), 'seq')  55.1 us
    all_gather x1, waiting for transfers between devices, body(): adapter_portion = lax.all_gather(value_down_map, 'seq', axis=0, tiled=True)  49.8 us
    all_gather x1, waiting for transfers between devices, body(): value_fragment = lax.all_gather(value_weight, 'seq', axis=0, tiled=True)  49.8 us
    all_gather x1, waiting for transfers between devices, body(): slots_all = lax.all_gather(attended, 'seq', axis=0, tiled=True)  38.3 us
  transfers between devices with their start and end apart: 11, of which 11 were waited for; matrix products, arithmetic and copies ran while one was open for 4% of the time, Pallas kernels for 0%

commit v1 on v0

--- a/solution.py
+++ b/solution.py
@@ -50,7 +50,14 @@
     group_heads = query_weight.shape[1] // head_dim
     every_row = jnp.concatenate([context, memory], axis=0)
     key_portion = lax.all_gather(key_weight, "seq", axis=0, tiled=True)
-    value_fragment = lax.all_gather(value_weight, "seq", axis=0, tiled=True)
+    size = lax.axis_size("seq")
+    route = [(i, (i + 1) % size) for i in range(size)]
+    terms = [value_weight]
+    for reach in range(1, size):
+        terms = [lax.ppermute(terms[0], "seq", route), *terms]
+    out = jnp.concatenate(terms, axis=0)
+    shift = (lax.axis_index("seq") + 1) * terms[-1].shape[0]
+    value_fragment = jnp.roll(out, shift, axis=0)
     adapter_portion = lax.all_gather(value_down_map, "seq", axis=0, tiled=True)
     combined_rows = jnp.concatenate([key_portion, value_fragment, adapter_portion], axis=1)
     projected = jnp.dot(every_row, combined_rows, preferred_element_type=jnp.float32)

time: 714 us -> 681 us (0.954)
  waiting for transfers between devices: 532 us -> 480 us
  local copies, waits for them, and re-layouts: 13 us -> 26.1 us
    ppermute x0 -> x7, waiting for transfers between devices: none -> 67.9 us  [body(): terms = [lax.ppermute(terms[0], 'seq', route), *terms]]
    all_gather x1 -> x0, waiting for transfers between devices: 49.8 us -> none  [body(): value_fragment = lax.all_gather(value_weight, 'seq', axis=0, tiled=True)]
    all_gather x1, waiting for transfers between devices: 49.8 us -> 14.3 us  [body(): adapter_portion = lax.all_gather(value_down_map, 'seq', axis=0, tiled=True)]
    all_gather x1, waiting for transfers between devices: 33.8 us -> 0.02 us  [body(): key_portion = lax.all_gather(key_weight, 'seq', axis=0, tiled=True)]
    unnamed x31 -> x72, local copies, waits for them, and re-layouts: 10.9 us -> 20.3 us
  transfers between devices with their start and end apart: 11 -> 17, of which waited for: 11 -> 16; matrix products, arithmetic and copies ran while one was open for 4% -> 6% of each run, Pallas kernels for 0% -> 0%
where the time goes in v1:
time: 681 us; the launch traced here: 680 us
  waiting for transfers between devices  480 us (70%)
  blocking collectives  97.8 us (14%)
  matrix products  46.1 us (7%)
  local copies, waits for them, and re-layouts  26.1 us (4%)
  between operations  14.7 us (2%)
  other arithmetic  10.9 us (2%)
    reduce_scatter x1, waiting for transfers between devices, body(): lax.psum_scatter(trailing_contract(grads_all, output_weight), 'seq', scat...  68.5 us
    ppermute x7, waiting for transfers between devices, body(): terms = [lax.ppermute(terms[0], 'seq', route), *terms]  67.9 us
    reduce_scatter x1, waiting for transfers between devices, body(): lax.psum_scatter(leading_contract(row_cols, value_backward), 'seq', scatt...  67.2 us
    reduce_scatter x1, waiting for transfers between devices, body(): lax.psum_scatter(leading_contract(memory_cols, query_backward), 'seq', sc...  67 us
    reduce_scatter x1, waiting for transfers between devices, body(): lax.psum_scatter(leading_contract(prob_low, grad_rows_local), 'seq', scat...  57.7 us
    psum x1, waiting for transfers between devices, body(): lax.psum((query_up_portion, value_up_portion), 'seq')  55.2 us
    all_gather x1, waiting for transfers between devices, body(): slots_all = lax.all_gather(attended, 'seq', axis=0, tiled=True)  38.6 us
    all_gather x1, blocking collectives, body(): lax.all_gather(keys_local, 'seq', axis=0, tiled=True)  32 us
  transfers between devices with their start and end apart: 17, of which 16 were waited for; matrix products, arithmetic and copies ran while one was open for 6% of the time, Pallas kernels for 0%

profile of v1, /device:TPU:0, one launch (start us, length us, event | category | flops | bytes accessed | tf_op | source)
XLA Modules:
  0.0 679.5 jit_solution(7779054535208200079)
XLA Ops:
  8.0 3.0 collective-permute-start
  11.0 9.6 %collective-permute-done = bf16[1024,128]{1,0:T(8,128)(2,1)S(1)} collective-permute-done((bf16[1024,128]{1,0:T(8,128)(2,1)}, bf16[1024,128]{1,0:T(8,128)(2,1)S(1)}, u32[]{:S(2)}, u32[]{:S(2)}) %collective-permute-start) | collective-permute-done | bytes 262176 | tf_op jit(solution)/shard_map/ppermute | solution.py:57
  20.7 15.9 %collective-permute-done.1 = bf16[1024,128]{1,0:T(8,128)(2,1)} collective-permute-done((bf16[1024,128]{1,0:T(8,128)(2,1)S(1)}, bf16[1024,128]{1,0:T(8,128)(2,1)}, u32[]{:S(2)}, u32[]{:S(2)}) %collective-permute-start.1) | collective-permute-done | bytes 262176 | tf_op jit(solution)/shard_map/ppermute | solution.py:57
  36.5 2.5 constant_dynamic-update-slice_fusion.1
  39.0 6.8 %collective-permute-done.2 = bf16[1024,128]{1,0:T(8,128)(2,1)S(1)} collective-permute-done((bf16[1024,128]{1,0:T(8,128)(2,1)}, bf16[1024,128]{1,0:T(8,128)(2,1)S(1)}, u32[]{:S(2)}, u32[]{:S(2)}) %collective-permute-start.2) | collective-permute-done | bytes 262176 | tf_op jit(solution)/shard_map/ppermute | solution.py:57
  46.5 15.8 %collective-permute-done.3 = bf16[1024,128]{1,0:T(8,128)(2,1)S(1)} collective-permute-done((bf16[1024,128]{1,0:T(8,128)(2,1)S(1)}, bf16[1024,128]{1,0:T(8,128)(2,1)S(1)}, u32[]{:S(2)}, u32[]{:S(2)}) %collective-permute-start.3) | collective-permute-done | bytes 262176 | tf_op jit(solution)/shard_map/ppermute | solution.py:57
  62.3 9.0 %fusion.18 = bf16[64,1024]{1,0:T(8,128)(2,1)S(1)} fusion(f32[64,1024]{1,0:T(8,128)S(1)} %convolution_multiply_fusion.1, bf16[64,8192]{1,0:T(8,128)(2,1)S(1)} %copy-done.2, bf16[8192,1024]{1,0:T(8,128)(2,1)} %param.15), kind=kOutput, calls=%fused_computation.25 | convolution fusion | flops 1073872896 | bytes 18219008 | tf_op jit(solution)/shard_map/dot_general | solution.py:69
  71.3 6.3 collective-permute-done.4
  77.7 2.3 copy-done.4
  81.2 8.4 %collective-permute-done.5 = bf16[1024,128]{1,0:T(8,128)(2,1)} collective-permute-done((bf16[1024,128]{1,0:T(8,128)(2,1)}, bf16[1024,128]{1,0:T(8,128)(2,1)}, u32[]{:S(2)}, u32[]{:S(2)}) %collective-permute-start.5) | collective-permute-done | bytes 262176 | tf_op jit(solution)/shard_map/ppermute | solution.py:57
  90.2 1.3 reduce-window.8
  91.5 1.3 broadcast_in_dim.5
  92.8 1.4 ge.31
  96.5 5.2 collective-permute-done.6
  103.8 1.0 constant_dynamic-update-slice_fusion.14
  104.8 1.0 constant_dynamic-update-slice_fusion.13
  111.0 1.4 constant_dynamic-slice_fusion
  112.5 14.3 %all-gather.7.cloned.1.call-done = bf16[8192,128]{1,0:T(8,128)(2,1)} async-done(((bf16[1024,128]{1,0:T(8,128)(2,1)}), bf16[8192,128]{1,0:T(8,128)(2,1)}) %all-gather.7.cloned.1.call-update) | async-done | bytes 2097168 | tf_op jit(solution)/shard_map/all_gather | solution.py:61
  126.9 7.2 %fusion.50 = (bf16[320,384]{1,0:T(8,128)(2,1)S(1)}, f32[320,384]{1,0:T(8,128)S(1)}) fusion(bf16[320,8192]{1,0:T(8,128)(2,1)} %copy-done.4, bf16[8192,128]{1,0:T(8,128)(2,1)} %all-gather.7.cloned.1.call-done, bf16[8192,128]{1,0:T(8,128)(2,1)} %constant_dynamic-slice_fusion, bf16[8192,128]{1,0:T(8,128)(2,1)} %all-gather.5.cloned.1.call-done), kind=kOutput, calls=%fused_computation.100 | convolution fusion | flops 2032263168 | bytes 12271616 | tf_op jit(solution)/shard_map/dot_general | solution.py:63
  134.1 32.0 %all_gather.20 = bf16[2560,128]{1,0:T(8,128)(2,1)S(1)} all-gather(bf16[320,128]{1,0:T(8,128)(2,1)S(1)} %slice.14), channel_id=1, replica_groups=mesh['section'=4,'seq'=8] {'seq'}, dimensions={0}, use_global_device_ids=true | all-gather | bytes 737280 | tf_op jit(solution)/shard_map/all_gather | solution.py:78
  166.3 31.9 %all_gather.21 = bf16[2560,128]{1,0:T(8,128)(2,1)S(1)} all-gather(bf16[320,128]{1,0:T(8,128)(2,1)S(1)} %fusion.24), channel_id=1, replica_groups=mesh['section'=4,'seq'=8] {'seq'}, dimensions={0}, use_global_device_ids=true | all-gather | bytes 737280 | tf_op jit(solution)/shard_map/all_gather | solution.py:79
  198.2 2.0 fusion.51
  201.0 1.3 fusion.6
  202.3 2.4 copy-done.1
  206.3 38.6 %all-gather.9.cloned.1.call-done = bf16[512,1024]{1,0:T(8,128)(2,1)} async-done(((bf16[64,1024]{1,0:T(8,128)(2,1)}), bf16[512,1024]{1,0:T(8,128)(2,1)}) %all-gather.9.cloned.1.call-update) | async-done | bytes 1048592 | tf_op jit(solution)/shard_map/all_gather | solution.py:111
  244.9 3.8 fusion.52
  248.8 30.0 %reduce-scatter.6.cloned.1.call-done = f32[128,1024]{1,0:T(8,128)} async-done(((f32[512,1024]{1,0:T(8,128)}), f32[128,1024]{1,0:T(8,128)}) %reduce-scatter.6.cloned.1.call-update) | async-done | bytes 524304 | tf_op jit(solution)/shard_map/reduce_scatter | solution.py:112
  278.8 1.2 multiply_reduce_fusion.1
  280.0 21.4 %all-reduce = (f32[128]{0:T(128)S(1)}, f32[128]{0:T(128)S(1)}) all-reduce(f32[128]{0:T(128)S(1)} %get-tuple-element.6, f32[128]{0:T(128)S(1)} %get-tuple-element.5), channel_id=1, replica_groups=mesh['section'=4,'seq'=8] {'seq'}, use_global_device_ids=true, to_apply=%region_7.8 | all-reduce | flops 256 | bytes 2048 | tf_op jit(solution)/shard_map/psum | solution.py:120
  301.4 2.0 subtract_convert_fusion
  303.5 13.1 %all-gather.11.cloned.1.call-done = bf16[512,1024]{1,0:T(8,128)(2,1)} async-done(((bf16[128,1024]{1,0:T(8,128)(2,1)}), bf16[512,1024]{1,0:T(8,128)(2,1)}) %all-gather.11.cloned.1.call-update) | async-done | bytes 1048592 | tf_op jit(solution)/shard_map/all_gather | solution.py:128
  316.6 3.9 fusion.53
  320.6 68.5 %reduce-scatter.8.cloned.1.call-done = f32[64,1024]{1,0:T(8,128)} async-done(((f32[512,1024]{1,0:T(8,128)}), f32[64,1024]{1,0:T(8,128)}) %reduce-scatter.8.cloned.1.call-update) | async-done | bytes 262160 | tf_op jit(solution)/shard_map/reduce_scatter | solution.py:129
  390.2 4.4 fusion.12
  394.7 3.8 multiply_reduce_fusion
  399.0 1.1 fusion.17
  400.1 1.0 convolution_multiply_fusion
  401.1 57.7 %reduce-scatter.12.cloned.1.call-done = f32[320,128]{1,0:T(8,128)} async-done(((f32[2560,128]{1,0:T(8,128)}), f32[320,128]{1,0:T(8,128)}) %reduce-scatter.12.cloned.1.call-update) | async-done | bytes 163856 | tf_op jit(solution)/shard_map/reduce_scatter | solution.py:141
  458.9 1.8 convolution_multiply_fusion.4
  461.0 1.1 convolution_multiply_fusion.2
  462.0 12.5 %all-reduce.7 = (bf16[64,128]{1,0:T(8,128)(2,1)S(1)}, bf16[320,128]{1,0:T(8,128)(2,1)S(1)}) all-reduce(f32[64,128]{1,0:T(8,128)S(1)} %convolution_multiply_fusion.5, f32[320,128]{1,0:T(8,128)S(1)} %convolution_multiply_fusion.2), channel_id=1, replica_groups=mesh['section'=4,'seq'=8] {'section'}, use_global_device_ids=true, to_apply=%region_12.13 | all-reduce | flops 49152 | bytes 294912 | tf_op jit(solution)/shard_map/psum | solution.py:149
  474.6 2.9 fusion.10
  477.6 2.3 fusion.22
  479.9 55.2 %all-reduce.6.cloned.1.call-done = (f32[128,1024]{1,0:T(8,128)}, f32[128,128]{1,0:T(8,128)}) async-done(((f32[128,1024]{1,0:T(8,128)}, f32[128,128]{1,0:T(8,128)}), (f32[128,1024]{1,0:T(8,128)}, f32[128,128]{1,0:T(8,128)})) %all-reduce.6.cloned.1.call-update) | async-done | bytes 589840 | tf_op jit(solution)/shard_map/psum | solution.py:146
  535.1 67.2 %reduce-scatter.14.cloned.1.call-done = f32[256,128]{1,0:T(8,128)} async-done(((f32[2048,128]{1,0:T(8,128)}), f32[256,128]{1,0:T(8,128)}) %reduce-scatter.14.cloned.1.call-update) | async-done | bytes 131088 | tf_op jit(solution)/shard_map/reduce_scatter | solution.py:165
  602.4 67.0 %reduce-scatter.10.cloned.1.call-done = f32[256,128]{1,0:T(8,128)} async-done(((f32[2048,128]{1,0:T(8,128)}), f32[256,128]{1,0:T(8,128)}) %reduce-scatter.10.cloned.1.call-update) | async-done | bytes 131088 | tf_op jit(solution)/shard_map/reduce_scatter | solution.py:162
  669.3 1.9 copy.40
  671.2 1.5 copy.41
  (114 shorter events, 17.7 us)
Async XLA Ops:
  7.2 237.7 %copy-start = (bf16[1024,1024]{1,0:T(8,128)(2,1)S(1)}, bf16[1024,1024]{1,0:T(8,128)(2,1)}, u32[]{:S(2)}) copy-start(bf16[1024,1024]{1,0:T(8,128)(2,1)} %param.22) | copy-start | bytes 6291460
  7.2 105.3 %all-gather.5.cloned.1.call-start = ((), (), s32[]{:S(2)}) async-start(), calls=%async_computation.5 | async-start | bytes 2359296 | tf_op jit(solution)/shard_map/all_gather | solution.py:52
  7.9 119.0 %all-gather.7.cloned.1.call-start = ((), (), s32[]{:S(2)}) async-start(), calls=%async_computation.6 | async-start | bytes 2359296 | tf_op jit(solution)/shard_map/all_gather | solution.py:61
  8.0 12.6 %collective-permute-start = (bf16[1024,128]{1,0:T(8,128)(2,1)}, bf16[1024,128]{1,0:T(8,128)(2,1)S(1)}, u32[]{:S(2)}, u32[]{:S(2)}) collective-permute-start(bf16[1024,128]{1,0:T(8,128)(2,1)} %param.17), channel_id=1, source_target_pairs={{0,1},{1,2},{2,3},{3,4},{4,5},{5,6},{6,7},{7,0},{8,9},{9,10},{10,1... | collective-permute-start | bytes 786440 | tf_op jit(solution)/shard_map/ppermute | solution.py:57
  20.5 18.5 %copy-start.9 = (bf16[1024,128]{1,0:T(8,128)(2,1)}, bf16[1024,128]{1,0:T(8,128)(2,1)S(1)}, u32[]{:S(2)}) copy-start(bf16[1024,128]{1,0:T(8,128)(2,1)S(1)} %collective-permute-done) | copy-start | bytes 786436
  20.5 16.0 %collective-permute-start.1 = (bf16[1024,128]{1,0:T(8,128)(2,1)S(1)}, bf16[1024,128]{1,0:T(8,128)(2,1)}, u32[]{:S(2)}, u32[]{:S(2)}) collective-permute-start(bf16[1024,128]{1,0:T(8,128)(2,1)S(1)} %collective-permute-done), channel_id=1, source_target_pairs={{0,1},{1,2},{2,3},{3,4},{4,5},{5,6},{6,7},{7,0},{8,9},{9,10},{10,1... | collective-permute-start | bytes 786440 | tf_op jit(solution)/shard_map/ppermute | solution.py:57
  20.6 25.3 %copy-start.2 = (bf16[64,8192]{1,0:T(8,128)(2,1)S(1)}, bf16[64,8192]{1,0:T(8,128)(2,1)}, u32[]{:S(2)}) copy-start(bf16[64,8192]{1,0:T(8,128)(2,1)} %param.14) | copy-start | bytes 3145732
  20.6 224.3 %all-gather.9.cloned.1.call-start = ((), (), s32[]{:S(2)}) async-start(), calls=%async_computation.7 | async-start | bytes 1179648 | tf_op jit(solution)/shard_map/all_gather | solution.py:111
  20.6 25.2 %copy-start.7 = (bf16[8192,128]{1,0:T(8,128)(2,1)S(1)}, bf16[8192,128]{1,0:T(8,128)(2,1)}, u32[]{:S(2)}) copy-start(bf16[8192,128]{1,0:T(8,128)(2,1)} %param.18) | copy-start | bytes 6291460
  20.6 25.7 %copy-start.15 = (bf16[128,1024]{1,0:T(8,128)(2,1)S(1)}, bf16[128,1024]{1,0:T(8,128)(2,1)}, u32[]{:S(2)}) copy-start(bf16[128,1024]{1,0:T(8,128)(2,1)} %param.19) | copy-start | bytes 786436
  36.5 9.3 %collective-permute-start.2 = (bf16[1024,128]{1,0:T(8,128)(2,1)}, bf16[1024,128]{1,0:T(8,128)(2,1)S(1)}, u32[]{:S(2)}, u32[]{:S(2)}) collective-permute-start(bf16[1024,128]{1,0:T(8,128)(2,1)} %collective-permute-done.1), channel_id=1, source_target_pairs={{0,1},{1,2},{2,3},{3,4},{4,5},{5,6},{6,7},{7,0},{8,9},{9,10},{10,1... | collective-permute-start | bytes 786440 | tf_op jit(solution)/shard_map/ppermute | solution.py:57
  45.8 25.5 %copy-start.11 = (bf16[1024,128]{1,0:T(8,128)(2,1)}, bf16[1024,128]{1,0:T(8,128)(2,1)S(1)}, u32[]{:S(2)}) copy-start(bf16[1024,128]{1,0:T(8,128)(2,1)S(1)} %collective-permute-done.2) | copy-start | bytes 786436
  45.8 16.5 %collective-permute-start.3 = (bf16[1024,128]{1,0:T(8,128)(2,1)S(1)}, bf16[1024,128]{1,0:T(8,128)(2,1)S(1)}, u32[]{:S(2)}, u32[]{:S(2)}) collective-permute-start(bf16[1024,128]{1,0:T(8,128)(2,1)S(1)} %collective-permute-done.2), channel_id=1, source_target_pairs={{0,1},{1,2},{2,3},{3,4},{4,5},{5,6},{6,7},{7,0},{8,9},{9,10},{10,1... | collective-permute-start | bytes 786440 | tf_op jit(solution)/shard_map/ppermute | solution.py:57
  62.3 9.0 %copy-start.13 = (bf16[1024,128]{1,0:T(8,128)(2,1)}, bf16[1024,128]{1,0:T(8,128)(2,1)S(1)}, u32[]{:S(2)}) copy-start(bf16[1024,128]{1,0:T(8,128)(2,1)S(1)} %collective-permute-done.3) | copy-start | bytes 786436
  62.3 15.3 %collective-permute-start.4 = (bf16[1024,128]{1,0:T(8,128)(2,1)S(1)}, bf16[1024,128]{1,0:T(8,128)(2,1)}, u32[]{:S(2)}, u32[]{:S(2)}) collective-permute-start(bf16[1024,128]{1,0:T(8,128)(2,1)S(1)} %collective-permute-done.3), channel_id=1, source_target_pairs={{0,1},{1,2},{2,3},{3,4},{4,5},{5,6},{6,7},{7,0},{8,9},{9,10},{10,1... | collective-permute-start | bytes 786440 | tf_op jit(solution)/shard_map/ppermute | solution.py:57
  71.3 36.5 %copy-start.8 = (bf16[1024,128]{1,0:T(8,128)(2,1)S(1)}, bf16[1024,128]{1,0:T(8,128)(2,1)}, u32[]{:S(2)}) copy-start(bf16[1024,128]{1,0:T(8,128)(2,1)} %param.17) | copy-start | bytes 786436
  77.6 12.1 %collective-permute-start.5 = (bf16[1024,128]{1,0:T(8,128)(2,1)}, bf16[1024,128]{1,0:T(8,128)(2,1)}, u32[]{:S(2)}, u32[]{:S(2)}) collective-permute-start(bf16[1024,128]{1,0:T(8,128)(2,1)} %collective-permute-done.4), channel_id=1, source_target_pairs={{0,1},{1,2},{2,3},{3,4},{4,5},{5,6},{6,7},{7,0},{8,9},{9,10},{10,1... | collective-permute-start | bytes 786440 | tf_op jit(solution)/shard_map/ppermute | solution.py:57
  77.7 2.3 copy-start.4
  80.0 29.8 %copy-start.14 = (bf16[1024,128]{1,0:T(8,128)(2,1)S(1)}, bf16[1024,128]{1,0:T(8,128)(2,1)}, u32[]{:S(2)}) copy-start(bf16[1024,128]{1,0:T(8,128)(2,1)} %copy-done.13) | copy-start | bytes 786436
  80.0 29.9 %copy-start.12 = (bf16[1024,128]{1,0:T(8,128)(2,1)S(1)}, bf16[1024,128]{1,0:T(8,128)(2,1)}, u32[]{:S(2)}) copy-start(bf16[1024,128]{1,0:T(8,128)(2,1)} %copy-done.11) | copy-start | bytes 786436
  80.0 30.9 %copy-start.10 = (bf16[1024,128]{1,0:T(8,128)(2,1)S(1)}, bf16[1024,128]{1,0:T(8,128)(2,1)}, u32[]{:S(2)}) copy-start(bf16[1024,128]{1,0:T(8,128)(2,1)} %copy-done.9) | copy-start | bytes 786436
  89.7 12.1 %collective-permute-start.6 = (bf16[1024,128]{1,0:T(8,128)(2,1)}, bf16[1024,128]{1,0:T(8,128)(2,1)S(1)}, u32[]{:S(2)}, u32[]{:S(2)}) collective-permute-start(bf16[1024,128]{1,0:T(8,128)(2,1)} %collective-permute-done.5), channel_id=1, source_target_pairs={{0,1},{1,2},{2,3},{3,4},{4,5},{5,6},{6,7},{7,0},{8,9},{9,10},{10,1... | collective-permute-start | bytes 786440 | tf_op jit(solution)/shard_map/ppermute | solution.py:57
  112.5 53.6 %copy-start.20 = (bf16[128,128]{1,0:T(8,128)(2,1)S(1)}, bf16[128,128]{1,0:T(8,128)(2,1)}, u32[]{:S(2)}) copy-start(bf16[128,128]{1,0:T(8,128)(2,1)} %param.21) | copy-start | bytes 98308
  112.5 85.6 %copy-start.19 = (bf16[512,128]{1,0:T(8,128)(2,1)S(1)}, bf16[512,128]{1,0:T(8,128)(2,1)}, u32[]{:S(2)}) copy-start(bf16[512,128]{1,0:T(8,128)(2,1)} %reshape.136) | copy-start | bytes 393220
  112.5 85.6 %copy-start.21 = (s32[2560]{0:T(1024)S(1)}, s32[2560]{0:T(1024)}, u32[]{:S(2)}) copy-start(s32[2560]{0:T(1024)} %fusion.38) | copy-start | bytes 30724
  112.5 85.6 %copy-start.23 = (s32[512]{0:T(512)S(1)}, s32[512]{0:T(512)}, u32[]{:S(2)}) copy-start(s32[512]{0:T(512)} %ge.31) | copy-start | bytes 6148
  112.5 85.6 %copy-start.24 = (pred[2560]{0:T(1024)(128)(4,1)S(1)}, pred[2560]{0:T(1024)(128)(4,1)}, u32[]{:S(2)}) copy-start(pred[2560]{0:T(1024)(128)(4,1)} %fusion.41) | copy-start | bytes 7684
  134.1 66.1 %copy-start.18 = (bf16[320,384]{1,0:T(8,128)(2,1)}, bf16[320,384]{1,0:T(8,128)(2,1)S(1)}, u32[]{:S(2)}) copy-start(bf16[320,384]{1,0:T(8,128)(2,1)S(1)} %get-tuple-element.17) | copy-start | bytes 737284
  166.1 34.1 %copy-start.5 = (bf16[2560,128]{1,0:T(8,128)(2,1)}, bf16[2560,128]{1,0:T(8,128)(2,1)S(1)}, u32[]{:S(2)}) copy-start(bf16[2560,128]{1,0:T(8,128)(2,1)S(1)} %all_gather.20) | copy-start | bytes 1966084
  198.2 4.2 copy-start.3
  202.3 2.4 copy-start.1
  206.3 42.5 %copy-start.22 = (f32[1024]{0:T(1024)S(1)}, f32[1024]{0:T(1024)}, u32[]{:S(2)}) copy-start(f32[1024]{0:T(1024)} %param.23) | copy-start | bytes 12292
  206.3 72.5 %copy-start.17 = (bf16[128,1024]{1,0:T(8,128)(2,1)S(1)}, bf16[128,1024]{1,0:T(8,128)(2,1)}, u32[]{:S(2)}) copy-start(bf16[128,1024]{1,0:T(8,128)(2,1)} %param.25) | copy-start | bytes 786436
  206.3 72.5 %reduce-scatter.6.cloned.1.call-start = ((), (), s32[]{:S(2)}) async-start(), calls=%async_computation.8 | async-start | bytes 2621440 | tf_op jit(solution)/shard_map/reduce_scatter | solution.py:112
  248.8 67.9 %all-gather.11.cloned.1.call-start = ((), (), s32[]{:S(2)}) async-start(), calls=%async_computation.9 | async-start | bytes 1310720 | tf_op jit(solution)/shard_map/all_gather | solution.py:128
  303.5 85.6 %reduce-scatter.8.cloned.1.call-start = ((), (), s32[]{:S(2)}) async-start(), calls=%async_computation.10 | async-start | bytes 2359296 | tf_op jit(solution)/shard_map/reduce_scatter | solution.py:129
  320.5 138.3 %reduce-scatter.12.cloned.1.call-start = ((), (), s32[]{:S(2)}) async-start(), calls=%async_computation.12 | async-start | bytes 1474560 | tf_op jit(solution)/shard_map/reduce_scatter | solution.py:141
  394.6 3.9 slice-start
  394.6 140.5 %all-reduce.6.cloned.1.call-start = ((), (), s32[]{:S(2)}) async-start(), calls=%async_computation.14 | async-start | bytes 1179648 | tf_op jit(solution)/shard_map/psum | solution.py:146
  394.7 4.2 slice-start.1
  394.7 4.3 copy-start.6
  399.0 61.8 %copy-start.16 = (bf16[128,1024]{1,0:T(8,128)(2,1)S(1)}, bf16[128,1024]{1,0:T(8,128)(2,1)}, u32[]{:S(2)}) copy-start(bf16[128,1024]{1,0:T(8,128)(2,1)} %param.19) | copy-start | bytes 786436
  460.7 141.7 %reduce-scatter.14.cloned.1.call-start = ((), (), s32[]{:S(2)}) async-start(), calls=%async_computation.13 | async-start | bytes 1179648 | tf_op jit(solution)/shard_map/reduce_scatter | solution.py:165
  477.6 191.8 %reduce-scatter.10.cloned.1.call-start = ((), (), s32[]{:S(2)}) async-start(), calls=%async_computation.11 | async-start | bytes 1179648 | tf_op jit(solution)/shard_map/reduce_scatter | solution.py:162
Sparse Core Ops, SparseCore 0:
  10.1 62.6 all-gather.4
  75.0 51.8 all-gather.6
  206.4 38.4 all-gather.8
  248.9 29.8 reduce-scatter.5
  303.6 13.0 all-gather.10
  320.6 68.4 reduce-scatter.7
  394.7 64.0 reduce-scatter.11
  462.8 72.2 all-reduce.5
  539.1 63.2 reduce-scatter.13
  606.2 63.1 reduce-scatter.9
